TPU v7x, 32 devices: a whole 2x2x4 slice. The times are simulated.
32 devices in a mesh: rep: 2 (over x), seq: 8 (over z, y), head: 2 (over core).
Axes of the slice: x: 2, y: 2, z: 4, core: 2. Of those that a mesh axis runs over, the one named last changes fastest.
Arguments:
- query_rows: bfloat16 [2048, 4096], P(('rep', 'seq'), 'head'), parts along dimension 0, may hold values from -40 to 40
- key_rows: bfloat16 [2048, 4096], P(('rep', 'seq'), 'head'), parts along dimension 0, may hold values from -6 to 6
- value_rows: bfloat16 [2048, 4096], P(('rep', 'seq'), 'head'), parts along dimension 0, may hold values from -6 to 6
- rand_blocks: int32 [16, 32, 3], P('rep'), parts along dimension 0, may hold values from 0 to 7, as said below
- out_weight: bfloat16 [4096, 4096], P('seq', 'head'), may hold values from -0.09375 to 0.09375
Outputs:
- projected: bfloat16 [2048, 4096], P(('rep', 'seq'), 'head'), parts along dimension 0
There are 2 independent parts, one for each index of `rep`. A program takes and returns all parts, laid end to end along the dimension named above; an argument that names none is the same for every part. Nothing has to cross between parts.
Inputs may be any that keep to these rules, and one draw needn't show every extreme that they name: `rand_blocks`: each entry is uniform over the blocks of the whole sequence. For the query blocks of one index of seq and the heads of one index of head, at most 6 entries name blocks held by one index of seq, and in every draw some index of seq is named exactly 6 times.
All inputs are finite; a program needn't handle non-finite values.
Results may differ from a plain program's by a relative error of at most 0.008.
Values may be sent and summed in bfloat16 or wider, within the bound.
No kernel may reach another device: no remote copies, remote signals or barrier semaphores. Data moves between devices by JAX's collectives and lax.ppermute only.
A program may use at most 128 MiB of HBM per device.

v0:
```python
import math
import jax
import jax.numpy as jnp
from jax import lax
from jax.sharding import PartitionSpec as P

HD = 128
BLK = 128
R = 3


def broadcast(block, axis, owner):
    block = jnp.where(lax.axis_index(axis) == owner, block, jnp.zeros_like(block))
    return lax.psum(block, axis)


def padded(array, sides, width):
    for axis, dim in sides:
        peers, length = (lax.axis_size(axis), array.shape[dim])
        up = [(i, (i + 1) % peers) for i in range(peers - 1)]
        down = [(j, i) for i, j in up]
        last = lax.slice_in_dim(array, length - width, length, axis=dim)
        initial = lax.slice_in_dim(array, 0, width, axis=dim)
        before = lax.ppermute(last, axis, up)
        after = lax.ppermute(initial, axis, down)
        array = jnp.concatenate([before, array, after], axis=dim)
    return array


def masked_softmax(scores, allowed):
    masked = jnp.where(allowed, scores, -jnp.inf)
    row_peak = jnp.max(masked, axis=-1, keepdims=True)
    expon_terms = jnp.where(allowed, jnp.exp(masked - row_peak), 0.0)
    return expon_terms / jnp.sum(expon_terms, axis=-1, keepdims=True)


def share_block(stacked, root_index):
    return broadcast(stacked, "seq", root_index)


def local(query_rows, key_rows, value_rows, rand_blocks, out_weight):
    tokens, features = query_rows.shape
    head_width = HD
    head_count = features // head_width
    blocks = tokens // BLK
    seq_count = lax.axis_size("seq")
    seq_index = lax.axis_index("seq")
    head_index = lax.axis_index("head")
    block_total = blocks * seq_count
    score_scale = 1.0 / math.sqrt(head_width)
    request_count = blocks * head_count * R
    slot_depth = (request_count + seq_count - 1) // seq_count
    first_rows = jnp.stack((query_rows, key_rows, value_rows))
    final_rows = jnp.stack((query_rows, key_rows, value_rows))
    first_glob = share_block(first_rows, 0)
    final_glob = share_block(final_rows, seq_count - 1)
    paired = jnp.stack((key_rows, value_rows))
    extended = padded(paired, (("seq", 1),), BLK)
    ext_heads = extended.reshape(2, blocks + 2, BLK, head_count, head_width).transpose(
        0, 3, 1, 2, 4
    )
    group_table = lax.dynamic_slice_in_dim(rand_blocks, head_index * head_count, head_count, 1)
    all_requests = group_table.reshape(seq_count, request_count)
    all_owner = all_requests // blocks
    request_order = jnp.arange(request_count, dtype=jnp.int32)
    earlier_request = request_order[None, :] < request_order[:, None]
    same_owner = all_owner[:, :, None] == all_owner[:, None, :]
    all_position = jnp.sum(same_owner & earlier_request[None], axis=2)
    owned_here = all_owner == seq_index
    slot_range = jnp.arange(slot_depth, dtype=jnp.int32)
    picked = owned_here[:, None, :] & (all_position[:, None, :] == slot_range[None, :, None])
    picked_request = jnp.sum(jnp.where(picked, request_order[None, None, :], 0), axis=2)
    picked_block = jnp.take_along_axis(all_requests, picked_request, axis=1) - seq_index * blocks
    picked_block = jnp.clip(picked_block, 0, blocks - 1).reshape(-1)
    picked_head = (picked_request // R % head_count).reshape(-1)
    local_pairs = paired.reshape(2, blocks, BLK, head_count, head_width)
    outgoing = local_pairs[:, picked_block, :, picked_head, :]
    outgoing = outgoing.reshape(seq_count, slot_depth, 2, BLK, head_width)
    received = lax.all_to_all(outgoing, "seq", split_axis=0, concat_axis=0, tiled=True)
    my_requests = lax.dynamic_slice_in_dim(all_requests, seq_index, 1, 0)[0]
    my_position = lax.dynamic_slice_in_dim(all_position, seq_index, 1, 0)[0]
    my_owner = my_requests // blocks
    rand_pairs = jnp.take(
        received.reshape(seq_count * slot_depth, 2, BLK, head_width),
        my_owner * slot_depth + my_position,
        axis=0,
    )
    rand_pairs = rand_pairs.reshape(blocks, head_count, R, 2, BLK, head_width).transpose(
        3, 1, 0, 2, 4, 5
    )
    block_ids = seq_index * blocks + jnp.arange(blocks, dtype=jnp.int32)
    base_slots = jnp.stack(
        [
            jnp.zeros((blocks,), jnp.int32),
            jnp.full((blocks,), block_total - 1, jnp.int32),
            jnp.clip(block_ids - 1, 0, block_total - 1),
            block_ids,
            jnp.clip(block_ids + 1, 0, block_total - 1),
        ],
        axis=1,
    )
    my_table = my_requests.reshape(blocks, head_count, R).transpose(1, 0, 2)
    slot_ids = jnp.concatenate(
        [jnp.broadcast_to(base_slots[None], (head_count, blocks, 5)), my_table], axis=2
    )
    slot_count = slot_ids.shape[2]
    equal_pair = slot_ids[:, :, :, None] == slot_ids[:, :, None, :]
    earlier = jnp.arange(slot_count)[None, :] < jnp.arange(slot_count)[:, None]
    slot_live = jnp.logical_not(jnp.any(equal_pair & earlier[None, None], axis=3))
    key_live = jnp.repeat(slot_live, BLK, axis=2)
    window_index = jnp.arange(blocks)[:, None] + jnp.arange(3)[None, :]
    query_heads = query_rows.reshape(blocks, BLK, head_count, head_width).transpose(2, 0, 1, 3)
    first_heads = first_glob.reshape(3, BLK, head_count, head_width).transpose(0, 2, 1, 3)
    final_heads = final_glob.reshape(3, BLK, head_count, head_width).transpose(0, 2, 1, 3)
    target_heads = max(1, 512 // (blocks * BLK))
    heads_step = max(
        (
            width
            for width in range(1, head_count + 1)
            if head_count % width == 0 and width <= target_heads
        )
    )

    def collect(ext_part, first_block, final_block, rand_part):
        steps_here = ext_part.shape[0]
        window_blocks = ext_part[:, window_index]
        glob_blocks = jnp.stack((first_block, final_block), axis=1)[:, None]
        joined = jnp.concatenate([glob_blocks, window_blocks, rand_part], axis=2)
        return joined.reshape(steps_here, blocks, slot_count * BLK, head_width)

    def attend(head_items):
        (
            query_one,
            key_ext,
            value_ext,
            key_first,
            value_first,
            key_final,
            value_final,
            key_rand,
            value_rand,
            live_one,
        ) = head_items
        keys_sel = collect(key_ext, key_first, key_final, key_rand)
        values_sel = collect(value_ext, value_first, value_final, value_rand)
        scores = (
            jnp.einsum("hibd,hikd->hibk", query_one, keys_sel, preferred_element_type=jnp.float32)
            * score_scale
        )
        weights = masked_softmax(scores, live_one[:, :, None, :]).astype(jnp.bfloat16)
        mixed = jnp.einsum(
            "hibk,hikd->hibd", weights, values_sel, preferred_element_type=jnp.float32
        )
        return mixed.astype(jnp.bfloat16)

    def split_heads(array):
        return array.reshape((head_count // heads_step, heads_step) + array.shape[1:])

    head_inputs = (
        query_heads,
        ext_heads[0],
        ext_heads[1],
        first_heads[1],
        first_heads[2],
        final_heads[1],
        final_heads[2],
        rand_pairs[0],
        rand_pairs[1],
        key_live,
    )
    block_heads = lax.map(attend, tuple((split_heads(item) for item in head_inputs)))
    block_heads = block_heads.reshape(head_count, blocks, BLK, head_width)
    attended = block_heads.transpose(1, 2, 0, 3).reshape(tokens, features)
    glob_query = jnp.concatenate((first_glob[0], final_glob[0]), axis=0).reshape(
        2 * BLK, head_count, head_width
    )
    key_heads = key_rows.reshape(tokens, head_count, head_width)
    value_wide = value_rows.reshape(tokens, head_count, head_width).astype(jnp.float32)
    glob_scores = (
        jnp.einsum("rhd,thd->hrt", glob_query, key_heads, preferred_element_type=jnp.float32)
        * score_scale
    )
    local_peak = jnp.max(glob_scores, axis=2)
    row_peak = lax.pmax(local_peak, "seq")
    expon_terms = jnp.exp(glob_scores - row_peak[:, :, None])
    denoms = jnp.sum(expon_terms, axis=2)
    numer_terms = jnp.einsum(
        "hrt,thd->hrd", expon_terms, value_wide, preferred_element_type=jnp.float32
    )
    numer_terms, denoms = lax.psum((numer_terms, denoms), "seq")
    glob_out = (
        (numer_terms / denoms[:, :, None])
        .astype(jnp.bfloat16)
        .transpose(1, 0, 2)
        .reshape(2 * BLK, features)
    )
    head_block = jnp.where(seq_index == 0, glob_out[:BLK], attended)
    attended = attended.at[:BLK].set(head_block)
    tail_block = jnp.where(seq_index == seq_count - 1, glob_out[BLK:], attended)
    attended = attended.at[tokens - BLK :].set(tail_block)
    partial_terms = lax.dot_general(
        lax.all_gather(out_weight, "seq", axis=0, tiled=True),
        attended,
        (((1,), (1,)), ((), ())),
        preferred_element_type=jnp.float32,
    )
    summed = lax.psum_scatter(
        partial_terms.astype(jnp.bfloat16), "head", scatter_dimension=0, tiled=True
    ).astype(jnp.float32)
    return summed.T.astype(jnp.bfloat16)


def solution(mesh):
    placed = (
        P(("rep", "seq"), "head"),
        P(("rep", "seq"), "head"),
        P(("rep", "seq"), "head"),
        P("rep", None, None),
        P("seq", "head"),
    )
    return jax.shard_map(
        local, mesh=mesh, in_specs=placed, out_specs=P(("rep", "seq"), "head"), check_vma=False
    )
```

profile of v0, /device:TPU:0, one launch (start us, length us, event | category | flops | bytes accessed | tf_op | source)
XLA Modules:
  0.0 597.0 jit_solution(8939532959045065275)
XLA Ops:
  9.7 1.9 broadcast_select_fusion
  11.8 132.2 %all-reduce.6.cloned.1.call-done = (bf16[3,128,2048]{1,2,0:T(8,128)(2,1)}, bf16[3,128,2048]{1,2,0:T(8,128)(2,1)}) async-done(((bf16[3,128,2048]{1,2,0:T(8,128)(2,1)}, bf16[3,128,2048]{1,2,0:T(8,128)(2,1)}), (bf16[3,128,2048]{1,2,0:T(8,128)(2,1)}, bf16[3,128,2048]{1,2,0:T(8,128)(2,1)})) %all-reduce.6.cloned.1.call-update) | async-done | bytes 3145744 | tf_op jit(solution)/shard_map/psum | solution.py:14
  150.0 35.1 %pmax.7 = f32[16,256]{1,0:T(8,128)S(1)} all-reduce(f32[16,256]{1,0:T(8,128)S(1)} %get-tuple-element.247), channel_id=1, replica_groups=mesh['rep'=2,'seq'=8,'head'=2] {'seq'}, use_global_device_ids=true, to_apply=%region_3.4 | all-reduce | flops 4096 | bytes 32768 | tf_op jit(solution)/shard_map/pmax | solution.py:184
  185.1 3.0 fusion.25
  194.4 2.8 gather_fusion.2
  197.2 4.6 all-to-all-start
  202.9 4.7 collective-permute-start
  213.0 35.9 %collective-permute-done = bf16[2,128,2048]{1,2,0:T(8,128)(2,1)} collective-permute-done((bf16[2,128,2048]{1,2,0:T(8,128)(2,1)}, bf16[2,128,2048]{1,2,0:T(8,128)(2,1)}, u32[]{:S(2)}, u32[]{:S(2)}) %collective-permute-start) | collective-permute-done | bytes 1048608 | tf_op jit(solution)/shard_map/ppermute | solution.py:24
  248.8 3.3 pad_maximum_fusion.2
  252.1 4.7 copy.100
  256.8 2.9 copy.128
  259.8 2.2 fusion.58
  263.1 2.1 fusion.59
  265.2 2.1 copy.99
  269.7 101.5 %psum.31 = f32[16,256]{1,0:T(8,128)S(1)} all-reduce(f32[16,256]{1,0:T(8,128)S(1)} %fusion.24), channel_id=1, replica_groups=mesh['rep'=2,'seq'=8,'head'=2] {'seq'}, use_global_device_ids=true, to_apply=%region_6.7 | all-reduce | flops 4096 | bytes 32768 | tf_op jit(solution)/shard_map/psum | solution.py:190
  375.4 3.1 gather_fusion.3
  380.3 49.2 %while.16 = (s32[]{:T(128)}, bf16[4,4,1,128,128]{3,4,1,0,2:T(8,128)(2,1)}, pred[4,4,1,1024]{3,1,2,0:T(4,128)(4,1)S(1)}, bf16[4,4,1,128,128]{4,3,1,2,0:T(8,128)(2...) while((s32[]{:T(128)}, ...), condition=%wide.region_13.14_spmd.clone.clone, body=%wide.region_10.13_spmd.clone.clone.sunk | while | flops 274532352 | bytes 33842396 | solution.py:171
  384.8 3.1 fusion.76
  397.1 3.1 fusion.76
  409.4 3.1 fusion.76
  421.7 3.1 fusion.76
  431.4 139.7 %all-gather.2.cloned.1.call-done = bf16[4096,2048]{1,0:T(8,128)(2,1)} async-done(((bf16[512,2048]{1,0:T(8,128)(2,1)}), bf16[4096,2048]{1,0:T(8,128)(2,1)}) %all-gather.2.cloned.1.call-update) | async-done | bytes 16777232 | tf_op jit(solution)/shard_map/all_gather | solution.py:202
  571.1 12.5 %fusion.22 = bf16[4096,128]{0,1:T(8,128)(2,1)} fusion(bf16[128,2048]{0,1:T(8,128)(2,1)S(1)} %fusion.37, bf16[4096,2048]{1,0:T(8,128)(2,1)} %all-gather.2.cloned.1.call-done), kind=kOutput, calls=%fused_computation.43 | convolution fusion | flops 2148007936 | bytes 18350080 | tf_op jit(solution)/shard_map/dot_general | solution.py:201
  583.6 6.9 %reduce-scatter.2.cloned.1.call-done = bf16[2048,128]{0,1:T(8,128)(2,1)} async-done(((bf16[4096,128]{0,1:T(8,128)(2,1)}), bf16[2048,128]{0,1:T(8,128)(2,1)}) %reduce-scatter.2.cloned.1.call-update) | async-done | bytes 524304 | tf_op jit(solution)/shard_map/reduce_scatter | solution.py:207
  (183 shorter events, 69.6 us)
Async XLA Ops:
  6.5 182.3 %copy-start = (s32[8,32,3]{1,0,2:T(8,128)S(1)}, s32[8,32,3]{1,0,2:T(8,128)}, u32[]{:S(2)}) copy-start(s32[8,32,3]{1,0,2:T(8,128)} %param.18) | copy-start | bytes 9220
  6.5 2.9 copy-start.6
  6.5 137.5 %all-reduce.6.cloned.1.call-start = ((), (), s32[]{:S(2)}) async-start(), calls=%async_computation.5 | async-start | bytes 6291456 | tf_op jit(solution)/shard_map/psum | solution.py:14
  7.9 183.0 %copy-start.2 = (bf16[128,2048]{0,1:T(8,128)(2,1)}, bf16[128,2048]{0,1:T(8,128)(2,1)S(1)}, u32[]{:S(2)}) copy-start(bf16[128,2048]{0,1:T(8,128)(2,1)S(1)} %copy.84) | copy-start | bytes 1572868
  9.4 182.5 %copy-start.4 = (bf16[128,2048]{0,1:T(8,128)(2,1)}, bf16[128,2048]{0,1:T(8,128)(2,1)S(1)}, u32[]{:S(2)}) copy-start(bf16[128,2048]{0,1:T(8,128)(2,1)S(1)} %copy.85) | copy-start | bytes 1572868
  11.7 359.5 %all-reduce.4.cloned.1.call-start = ((), (), s32[]{:S(2)}) async-start(), calls=%async_computation.2 | async-start | bytes 4194304 | tf_op jit(solution)/shard_map/psum | solution.py:190
  188.1 382.9 %all-gather.2.cloned.1.call-start = ((), (), s32[]{:S(2)}) async-start(), calls=%async_computation.3 | async-start | bytes 18874368 | tf_op jit(solution)/shard_map/all_gather | solution.py:202
  197.2 4.6 copy-start.3
  197.2 4.6 copy-start.5
  197.2 178.2 %all-to-all-start = ((bf16[8,6,2,128,128]{4,3,2,1,0:T(8,128)(2,1)}), bf16[8,6,2,128,128]{4,3,2,1,0:T(8,128)(2,1)}, u32[]{:S(2)}, u32[]{:S(2)}) async-start(bf16[8,6,2,128,128]{4,3,2,1,0:T(8,128)(2,1)} %bitcast.194), calls=%async_computation | async-start | bytes 6291456 | tf_op jit(solution)/shard_map/all_to_all | solution.py:79
  201.7 388.7 %reduce-scatter.2.cloned.1.call-start = ((), (), s32[]{:S(2)}) async-start(), calls=%async_computation.4 | async-start | bytes 1572864 | tf_op jit(solution)/shard_map/reduce_scatter | solution.py:207
  202.9 45.9 %collective-permute-start = (bf16[2,128,2048]{1,2,0:T(8,128)(2,1)}, bf16[2,128,2048]{1,2,0:T(8,128)(2,1)}, u32[]{:S(2)}, u32[]{:S(2)}) collective-permute-start(bf16[2,128,2048]{1,2,0:T(8,128)(2,1)} %pad_maximum_fusion.4), channel_id=1, source_target_pairs={{0,2},{2,4},{4,6},{6,8},{8,10},{10,12},{12,14},{1,3},{3,5},{5,7},{... | collective-permute-start | bytes 3145736 | tf_op jit(solution)/shard_map/ppermute | solution.py:24
  207.6 41.2 %collective-permute-start.1 = (bf16[2,128,2048]{1,2,0:T(8,128)(2,1)}, bf16[2,128,2048]{1,2,0:T(8,128)(2,1)}, u32[]{:S(2)}, u32[]{:S(2)}) collective-permute-start(bf16[2,128,2048]{1,2,0:T(8,128)(2,1)} %pad_maximum_fusion.4), channel_id=1, source_target_pairs={{2,0},{4,2},{6,4},{8,6},{10,8},{12,10},{14,12},{3,1},{5,3},{7,5},{... | collective-permute-start | bytes 3145736 | tf_op jit(solution)/shard_map/ppermute | solution.py:25
  259.7 2.3 copy-start.7
  389.7 1.6 copy-start.8
  402.0 1.6 copy-start.8
  414.3 1.6 copy-start.8
  426.6 1.6 copy-start.8
  571.1 19.4 %copy-start.1 = (s32[8,32,3]{1,0,2:T(8,128)S(1)}, s32[8,32,3]{1,0,2:T(8,128)}, u32[]{:S(2)}) copy-start(s32[8,32,3]{1,0,2:T(8,128)} %param.18) | copy-start | bytes 9220
Sparse Core Ops, SparseCore 0:
  11.8 132.1 all-reduce.5
  188.3 152.7 all-reduce.3
  343.4 227.6 all-gather.1
  583.7 6.7 reduce-scatter.1
where the time goes:
time: 599 us; the launch traced here: 597 us
  waiting for transfers between devices  315 us (53%)
  blocking collectives  137 us (23%)
  local copies, waits for them, and re-layouts  73.9 us (12%)
  matrix products  31.6 us (5%)
  other arithmetic  14.8 us (2%)
  between operations  13.4 us (2%)
  starting transfers between devices  10.7 us (2%)
    all_gather x1, waiting for transfers between devices, local(): lax.all_gather(out_weight, 'seq', axis=0, tiled=True)  140 us
    psum x1, waiting for transfers between devices, broadcast(): return lax.psum(block, axis)  132 us
    psum x1, blocking collectives, local(): numer_terms, denoms = lax.psum((numer_terms, denoms), 'seq')  102 us
    ppermute x1, waiting for transfers between devices, padded(): before = lax.ppermute(last, axis, up)  35.9 us
    pmax x1, blocking collectives, local(): row_peak = lax.pmax(local_peak, 'seq')  35.1 us
    dot_general x1, matrix products, local(): lax.dot_general(lax.all_gather(out_weight, 'seq', axis=0, tiled=True), at...  12.5 us
    sub x4, matrix products, masked_softmax(): expon_terms = jnp.where(allowed, jnp.exp(masked - row_peak), 0.0)  12.3 us
  transfers between devices with their start and end apart: 7, of which 4 were waited for; matrix products, arithmetic and copies ran while one was open for 15% of the time, Pallas kernels for 0%

commit v1 on v0

--- a/solution.py
+++ b/solution.py
@@ -7,6 +7,18 @@
 HD = 128
 BLK = 128
 R = 3
+
+
+def doubled_up(x, axis, dim):
+    ways, here = (lax.axis_size(axis), lax.axis_index(axis))
+    grown, reach = (x, 1)
+    while reach < ways:
+        theirs = lax.ppermute(grown, axis, [(d, d ^ reach) for d in range(ways)])
+        mine_first = jnp.concatenate([grown, theirs], axis=dim)
+        theirs_first = jnp.concatenate([theirs, grown], axis=dim)
+        grown = jnp.where(here & reach == 0, mine_first, theirs_first)
+        reach = 2 * reach
+    return grown
 
 
 def broadcast(block, axis, owner):
@@ -199,7 +211,7 @@
     tail_block = jnp.where(seq_index == seq_count - 1, glob_out[BLK:], attended)
     attended = attended.at[tokens - BLK :].set(tail_block)
     partial_terms = lax.dot_general(
-        lax.all_gather(out_weight, "seq", axis=0, tiled=True),
+        doubled_up(out_weight, "seq", 0),
         attended,
         (((1,), (1,)), ((), ())),
         preferred_element_type=jnp.float32,

time: 599 us -> 818 us (1.37)
  waiting for transfers between devices: 315 us -> 564 us
  blocking collectives: 137 us -> 81.7 us
  other arithmetic: 14.8 us -> 28.1 us
    ppermute x0 -> x3, waiting for transfers between devices: none -> 356 us  [doubled_up(): theirs = lax.ppermute(grown, axis, [(d, d ^ reach) for d in range(ways)])]
    all_gather x1 -> x0, waiting for transfers between devices: 140 us -> none  [local(): lax.all_gather(out_weight, 'seq', axis=0, tiled=True)]
    psum x1, blocking collectives: 102 us -> 33.4 us  [local(): numer_terms, denoms = lax.psum((numer_terms, denoms), 'seq')]
    psum x1, waiting for transfers between devices: 0.01 us -> 44.3 us  [local(): numer_terms, denoms = lax.psum((numer_terms, denoms), 'seq')]
    ppermute x1, waiting for transfers between devices: 35.9 us -> 0.01 us  [padded(): before = lax.ppermute(last, axis, up)]
    psum x1, waiting for transfers between devices: 132 us -> 156 us  [broadcast(): return lax.psum(block, axis)]
    select_n x0 -> x2, other arithmetic: none -> 15.3 us  [doubled_up(): grown = jnp.where(here & reach == 0, mine_first, theirs_first)]
    pmax x1, blocking collectives: 35.1 us -> 48.3 us  [local(): row_peak = lax.pmax(local_peak, 'seq')]
  transfers between devices with their start and end apart: 7 -> 9, of which waited for: 4 -> 5; matrix products, arithmetic and copies ran while one was open for 15% -> 14% of each run, Pallas kernels for 0% -> 0%
where the time goes in v1:
time: 818 us; the launch traced here: 817 us
  waiting for transfers between devices  564 us (69%)
  blocking collectives  81.7 us (10%)
  local copies, waits for them, and re-layouts  72.2 us (9%)
  matrix products  39 us (5%)
  other arithmetic  28.1 us (3%)
  starting transfers between devices  17.5 us (2%)
  between operations  13.4 us (2%)
    ppermute x3, waiting for transfers between devices, doubled_up(): theirs = lax.ppermute(grown, axis, [(d, d ^ reach) for d in range(ways)])  356 us
    psum x1, waiting for transfers between devices, broadcast(): return lax.psum(block, axis)  156 us
    pmax x1, blocking collectives, local(): row_peak = lax.pmax(local_peak, 'seq')  48.3 us
    psum x1, waiting for transfers between devices, local(): numer_terms, denoms = lax.psum((numer_terms, denoms), 'seq')  44.3 us
    psum x1, blocking collectives, local(): numer_terms, denoms = lax.psum((numer_terms, denoms), 'seq')  33.4 us
  transfers between devices with their start and end apart: 9, of which 5 were waited for; matrix products, arithmetic and copies ran while one was open for 14% of the time, Pallas kernels for 0%

profile of v1, /device:TPU:0, one launch (start us, length us, event | category | flops | bytes accessed | tf_op | source)
XLA Modules:
  0.0 816.9 jit_solution(15466783843805708800)
XLA Ops:
  6.5 3.0 collective-permute-start
  18.3 2.8 gather_fusion.2
  21.1 5.1 all-to-all-start
  28.6 5.5 collective-permute-start.3
  35.6 49.7 %collective-permute-done = bf16[512,2048]{1,0:T(8,128)(2,1)} collective-permute-done((bf16[512,2048]{1,0:T(8,128)(2,1)}, bf16[512,2048]{1,0:T(8,128)(2,1)}, u32[]{:S(2)}, u32[]{:S(2)}) %collective-permute-start) | collective-permute-done | bytes 2097184 | tf_op jit(solution)/shard_map/ppermute | solution.py:16
  85.3 5.3 maximum_select_fusion.5
  91.0 155.5 %all-reduce.6.cloned.1.call-done = (bf16[3,128,2048]{1,2,0:T(8,128)(2,1)}, bf16[3,128,2048]{1,2,0:T(8,128)(2,1)}) async-done(((bf16[3,128,2048]{1,2,0:T(8,128)(2,1)}, bf16[3,128,2048]{1,2,0:T(8,128)(2,1)}), (bf16[3,128,2048]{1,2,0:T(8,128)(2,1)}, bf16[3,128,2048]{1,2,0:T(8,128)(2,1)})) %all-reduce.6.cloned.1.call-update) | async-done | bytes 3145744 | tf_op jit(solution)/shard_map/psum | solution.py:26
  252.5 48.3 %pmax.7 = f32[16,256]{1,0:T(8,128)S(1)} all-reduce(f32[16,256]{1,0:T(8,128)S(1)} %get-tuple-element.247), channel_id=1, replica_groups=mesh['rep'=2,'seq'=8,'head'=2] {'seq'}, use_global_device_ids=true, to_apply=%region_3.4 | all-reduce | flops 4096 | bytes 32768 | tf_op jit(solution)/shard_map/pmax | solution.py:196
  300.8 3.0 fusion.32
  307.1 3.2 pad_maximum_fusion.2
  310.2 4.7 copy.103
  314.9 2.9 copy.132
  326.0 33.4 %psum.31 = f32[16,256]{1,0:T(8,128)S(1)} all-reduce(f32[16,256]{1,0:T(8,128)S(1)} %fusion.31), channel_id=1, replica_groups=mesh['rep'=2,'seq'=8,'head'=2] {'seq'}, use_global_device_ids=true, to_apply=%region_6.7 | all-reduce | flops 4096 | bytes 32768 | tf_op jit(solution)/shard_map/psum | solution.py:202
  359.4 44.3 %all-reduce.4.cloned.1.call-done = f32[16,256,128]{2,1,0:T(8,128)} async-done(((f32[16,256,128]{2,1,0:T(8,128)}), f32[16,256,128]{2,1,0:T(8,128)}) %all-reduce.4.cloned.1.call-update) | async-done | bytes 2097168 | tf_op jit(solution)/shard_map/psum | solution.py:202
  407.9 3.0 gather_fusion.3
  413.2 10.0 %maximum_select_fusion.2 = bf16[2048,2048]{1,0:T(8,128)(2,1)} fusion(bf16[1024,2048]{1,0:T(8,128)(2,1)} %collective-permute-done.1, bf16[1024,2048]{1,0:T(8,128)(2,1)} %maximum_select_fusion.5, pred[]{:T(512)S(6)} %eq.79), kind=kLoop, calls=%fused_computation.50 | loop fusion | flops 37748736 | bytes 16777216 | tf_op jit(solution)/shard_map/jit(_where)/select_n | solution.py:19
  425.3 53.2 %while.16 = (s32[]{:T(128)}, bf16[4,4,1,128,128]{3,4,1,0,2:T(8,128)(2,1)}, pred[4,4,1,1024]{3,1,2,0:T(4,128)(4,1)}, bf16[4,4,1,128,128]{4,3,1,2,0:T(8,128)(2,1)}...) while((s32[]{:T(128)}, ...), condition=%wide.region_13.14_spmd.clone.clone, body=%wide.region_10.13_spmd.clone.clone.sunk | while | flops 274532352 | bytes 25452752 | solution.py:183
  432.7 3.1 fusion.83
  446.0 3.1 fusion.83
  459.3 3.1 fusion.83
  472.5 3.1 fusion.83
  479.8 306.3 %collective-permute-done.2 = bf16[2048,2048]{1,0:T(8,128)(2,1)} collective-permute-done((bf16[2048,2048]{1,0:T(8,128)(2,1)}, bf16[2048,2048]{1,0:T(8,128)(2,1)}, u32[]{:S(2)}, u32[]{:S(2)}) %collective-permute-start.2) | collective-permute-done | bytes 8388640 | tf_op jit(solution)/shard_map/ppermute | solution.py:16
  786.1 13.5 %fusion.29 = bf16[4096,128]{1,0:T(8,128)(2,1)} fusion(bf16[128,2048]{0,1:T(8,128)(2,1)S(1)} %fusion.44, bf16[2048,2048]{1,0:T(8,128)(2,1)} %collective-permute-done.2, bf16[2048,2048]{1,0:T(8,128)(2,1)} %maximum_select_fusion.2, pred[]{:T(512)S(6)} %eq.78), kind=kOutput, calls=%fused_computation.51 | convolution fusion | flops 2223505408 | bytes 18350080 | tf_op jit(solution)/shard_map/dot_general | solution.py:213
  799.6 8.7 %reduce-scatter.2.cloned.1.call-done = bf16[2048,128]{1,0:T(8,128)(2,1)} async-done(((bf16[4096,128]{1,0:T(8,128)(2,1)}), bf16[2048,128]{1,0:T(8,128)(2,1)}) %reduce-scatter.2.cloned.1.call-update) | async-done | bytes 524304 | tf_op jit(solution)/shard_map/reduce_scatter | solution.py:219
  (175 shorter events, 82.6 us)
Async XLA Ops:
  6.5 8.9 %copy-start = (s32[8,32,3]{1,0,2:T(8,128)S(1)}, s32[8,32,3]{1,0,2:T(8,128)}, u32[]{:S(2)}) copy-start(s32[8,32,3]{1,0,2:T(8,128)} %param.18) | copy-start | bytes 9220
  6.5 239.9 %all-reduce.6.cloned.1.call-start = ((), (), s32[]{:S(2)}) async-start(), calls=%async_computation.4 | async-start | bytes 6291456 | tf_op jit(solution)/shard_map/psum | solution.py:26
  6.5 78.7 %collective-permute-start = (bf16[512,2048]{1,0:T(8,128)(2,1)}, bf16[512,2048]{1,0:T(8,128)(2,1)}, u32[]{:S(2)}, u32[]{:S(2)}) collective-permute-start(bf16[512,2048]{1,0:T(8,128)(2,1)} %param.19), channel_id=1, source_target_pairs={{0,2},{2,0},{4,6},{6,4},{8,10},{10,8},{12,14},{14,12},{1,3},{3,1},... | collective-permute-start | bytes 6291464 | tf_op jit(solution)/shard_map/ppermute | solution.py:16
  21.1 64.2 %copy-start.3 = (bf16[512,2048]{1,0:T(8,128)(2,1)S(1)}, bf16[512,2048]{1,0:T(8,128)(2,1)}, u32[]{:S(2)}) copy-start(bf16[512,2048]{1,0:T(8,128)(2,1)} %param.19) | copy-start | bytes 6291460
  21.1 386.8 %all-to-all-start = ((bf16[8,6,2,128,128]{4,3,2,1,0:T(8,128)(2,1)}), bf16[8,6,2,128,128]{4,3,2,1,0:T(8,128)(2,1)}, u32[]{:S(2)}, u32[]{:S(2)}) async-start(bf16[8,6,2,128,128]{4,3,2,1,0:T(8,128)(2,1)} %bitcast.191), calls=%async_computation | async-start | bytes 6291456 | tf_op jit(solution)/shard_map/all_to_all | solution.py:91
  26.2 377.4 %all-reduce.4.cloned.1.call-start = ((), (), s32[]{:S(2)}) async-start(), calls=%async_computation.2 | async-start | bytes 4194304 | tf_op jit(solution)/shard_map/psum | solution.py:202
  27.3 279.7 %collective-permute-start.4 = (bf16[2,128,2048]{1,2,0:T(8,128)(2,1)}, bf16[2,128,2048]{1,2,0:T(8,128)(2,1)}, u32[]{:S(2)}, u32[]{:S(2)}) collective-permute-start(bf16[2,128,2048]{1,2,0:T(8,128)(2,1)} %pad_maximum_fusion.4), channel_id=1, source_target_pairs={{2,0},{4,2},{6,4},{8,6},{10,8},{12,10},{14,12},{3,1},{5,3},{7,5},{... | collective-permute-start | bytes 3145736 | tf_op jit(solution)/shard_map/ppermute | solution.py:37
  28.6 278.4 %collective-permute-start.3 = (bf16[2,128,2048]{1,2,0:T(8,128)(2,1)}, bf16[2,128,2048]{1,2,0:T(8,128)(2,1)}, u32[]{:S(2)}, u32[]{:S(2)}) collective-permute-start(bf16[2,128,2048]{1,2,0:T(8,128)(2,1)} %pad_maximum_fusion.4), channel_id=1, source_target_pairs={{0,2},{2,4},{4,6},{6,8},{8,10},{10,12},{12,14},{1,3},{3,5},{5,7},{... | collective-permute-start | bytes 3145736 | tf_op jit(solution)/shard_map/ppermute | solution.py:36
  90.6 322.6 %collective-permute-start.1 = (bf16[1024,2048]{1,0:T(8,128)(2,1)}, bf16[1024,2048]{1,0:T(8,128)(2,1)}, u32[]{:S(2)}, u32[]{:S(2)}) collective-permute-start(bf16[1024,2048]{1,0:T(8,128)(2,1)} %maximum_select_fusion.5), channel_id=1, source_target_pairs={{0,4},{2,6},{4,0},{6,2},{8,12},{10,14},{12,8},{14,10},{1,5},{3,7},... | collective-permute-start | bytes 12582920 | tf_op jit(solution)/shard_map/ppermute | solution.py:16
  303.9 504.5 %reduce-scatter.2.cloned.1.call-start = ((), (), s32[]{:S(2)}) async-start(), calls=%async_computation.3 | async-start | bytes 1572864 | tf_op jit(solution)/shard_map/reduce_scatter | solution.py:219
  317.8 2.2 copy-start.4
  423.2 362.9 %collective-permute-start.2 = (bf16[2048,2048]{1,0:T(8,128)(2,1)}, bf16[2048,2048]{1,0:T(8,128)(2,1)}, u32[]{:S(2)}, u32[]{:S(2)}) collective-permute-start(bf16[2048,2048]{1,0:T(8,128)(2,1)} %maximum_select_fusion.2), channel_id=1, source_target_pairs={{0,8},{2,10},{4,12},{6,14},{8,0},{10,2},{12,4},{14,6},{1,9},{3,11}... | collective-permute-start | bytes 25165832 | tf_op jit(solution)/shard_map/ppermute | solution.py:16
  425.3 53.2 %copy-start.2 = (bf16[128,16,128]{0,2,1:T(8,128)(2,1)S(1)}, bf16[128,16,128]{0,2,1:T(8,128)(2,1)}, u32[]{:S(2)}) copy-start(bf16[128,16,128]{0,2,1:T(8,128)(2,1)} %copy.94) | copy-start | bytes 1572868
  786.1 24.2 %copy-start.1 = (s32[8,32,3]{1,0,2:T(8,128)S(1)}, s32[8,32,3]{1,0,2:T(8,128)}, u32[]{:S(2)}) copy-start(s32[8,32,3]{1,0,2:T(8,128)} %param.18) | copy-start | bytes 9220
Sparse Core Ops, SparseCore 0:
  15.6 230.8 all-reduce.5
  304.0 99.6 all-reduce.3
  799.7 8.5 reduce-scatter.1
